TPU v7x, 32 devices: a whole 2x2x4 slice. The times are simulated.
32 devices in a mesh: dp: 2 (over y), ctx: 4 (over x, core), tensor: 4 (over z).
Axes of the slice: x: 2, y: 2, z: 4, core: 2. Of those that a mesh axis runs over, the one named last changes fastest.
Arguments:
- residual: bfloat16 [2048, 3584], P(('dp', 'ctx', 'tensor')), parts along dimension 0, may hold values from -6 to 6
- queries: bfloat16 [2048, 1024], P(('dp', 'ctx'), 'tensor'), parts along dimension 0, may hold values from -8 to 8
- key_heads: bfloat16 [2048, 512], P(('dp', 'ctx'), 'tensor'), parts along dimension 0, may hold values from -8 to 8
- value_heads: bfloat16 [2048, 512], P(('dp', 'ctx'), 'tensor'), parts along dimension 0, may hold values from -6 to 6
- doc_blocks: int32 [12], P('dp'), parts along dimension 0, may hold values from 1 to 16, 32 in all
- out_weight: bfloat16 [1024, 3584], P('tensor'), may hold values from -0.53125 to 0.53125
- post_gain: float32 [3584], replicated, may hold values from 0.1 to 1.9
- ffn_gain: float32 [3584], replicated, may hold values from 0.1 to 1.9
- gate_weight: bfloat16 [3584, 3584], P('ctx', 'tensor'), may hold values from -0.09375 to 0.09375
- up_weight: bfloat16 [3584, 3584], P('ctx', 'tensor'), may hold values from -0.09375 to 0.09375
Outputs:
- mixed_stream: bfloat16 [2048, 3584], P(('dp', 'ctx', 'tensor')), parts along dimension 0
- ffn_hidden: bfloat16 [2048, 3584], P(('dp', 'ctx'), 'tensor'), parts along dimension 0
There are 2 independent parts, one for each index of `dp`. A program takes and returns all parts, laid end to end along the dimension named above; an argument that names none is the same for every part. Nothing has to cross between parts.
Inputs may be any that keep to these rules, and one draw needn't show every extreme that they name: `doc_blocks`: the lengths, in blocks of 32 positions, of the 6 documents packed in order into the sequence; they sum to 32, and the longest has exactly 16 blocks.
All inputs are finite; a program needn't handle non-finite values.
Results may differ from a plain program's by a relative error of at most 0.025.
Values may be sent and summed in bfloat16 or wider, within the bound.
A program may use at most 64 MiB of HBM per device.

v0:
```python
import jax
import jax.numpy as jnp
from jax import lax
from jax.sharding import PartitionSpec as P

BLOCK = 32
SOFT_CAP = 50.0
NORM_EPS = 1e-06
ROPE_BASE = 10000.0


def partner_2(value, axis, apart):
    mask = 2**apart
    pairs = [(source, source ^ mask) for source in range(lax.axis_size(axis))]
    return lax.ppermute(value, axis, pairs)


def rope_angles(positions, head_size):
    halfway = head_size // 2
    frequency = ROPE_BASE ** (-(jnp.arange(halfway, dtype=jnp.float32) * 2.0) / head_size)
    angles = positions.astype(jnp.float32)[:, None] * frequency[None, :]
    return (jnp.cos(angles), jnp.sin(angles))


def rotate(heads_in, cosine, sine_value, head_size):
    rows_here = heads_in.shape[0]
    reshaped = heads_in.astype(jnp.float32).reshape(rows_here, -1, head_size)
    leading = reshaped[:, :, : head_size // 2]
    trailing = reshaped[:, :, head_size // 2 :]
    cos_wide = cosine[:, None, :]
    sin_wide = sine_value[:, None, :]
    turned = jnp.concatenate(
        [leading * cos_wide - trailing * sin_wide, trailing * cos_wide + leading * sin_wide], axis=2
    )
    return turned.reshape(rows_here, -1).astype(jnp.bfloat16)


def doc_of(positions, doc_blocks):
    doc_ends = jnp.cumsum(doc_blocks)
    passed = positions[:, None] // BLOCK >= doc_ends[None, :]
    return jnp.sum(passed.astype(jnp.int32), axis=1)


def rms_scale(values):
    return values * lax.rsqrt(jnp.mean(values * values, axis=-1, keepdims=True) + NORM_EPS)


def gelu_gate(gate_sum, up_sum):
    return (jax.nn.gelu(gate_sum, approximate=True) * up_sum).astype(jnp.bfloat16)


def attend(query_rows, query_pos, query_doc, key_rows, value_rows, key_pos, key_doc, score_scale):
    scores = (
        lax.dot_general(
            query_rows, key_rows, (((1,), (1,)), ((), ())), preferred_element_type=jnp.float32
        )
        * score_scale
    )
    capped = SOFT_CAP * jnp.tanh(scores / SOFT_CAP)
    visible = (key_pos[None, :] <= query_pos[:, None]) & (key_doc[None, :] == query_doc[:, None])
    weights = jnp.where(visible, jnp.exp(capped), 0.0).astype(jnp.bfloat16)
    numerator = jnp.dot(weights, value_rows, preferred_element_type=jnp.float32)
    denominator = jnp.sum(weights.astype(jnp.float32), axis=1)
    return (numerator, denominator)


def join_halves(own_part, other_part, own_first):
    return jnp.where(
        own_first,
        jnp.concatenate([own_part, other_part], axis=2),
        jnp.concatenate([other_part, own_part], axis=2),
    )


def per_device(
    residual,
    queries,
    key_heads,
    value_heads,
    doc_blocks,
    out_weight,
    post_gain,
    ffn_gain,
    gate_weight,
    up_weight,
):
    tok_rows = queries.shape[0]
    head_size = queries.shape[1]
    score_scale = head_size ** (-0.5)
    query_pos = lax.axis_index("ctx") * tok_rows + jnp.arange(tok_rows, dtype=jnp.int32)
    query_doc = doc_of(query_pos, doc_blocks)
    cosine, sine_value = rope_angles(query_pos, head_size)
    query_rot = rotate(queries, cosine, sine_value, head_size)
    stacked = jnp.stack([key_heads, value_heads])
    own_first = lax.axis_index("tensor") % 2 == 0
    partner = partner_2(stacked, "tensor", 0)
    joined = join_halves(stacked, partner, own_first)
    key_rot = rotate(joined[0], cosine, sine_value, head_size)
    shard_pair = (
        lax.all_gather(key_rot, "ctx", axis=0, tiled=True),
        lax.all_gather(joined[1], "ctx", axis=0, tiled=True),
    )
    key_pos = jnp.arange(shard_pair[0].shape[0], dtype=jnp.int32)
    numerator, denominator = attend(
        query_rot,
        query_pos,
        query_doc,
        shard_pair[0],
        shard_pair[1],
        key_pos,
        doc_of(key_pos, doc_blocks),
        score_scale,
    )
    attended = (numerator / denominator[:, None]).astype(jnp.bfloat16)
    attn_rows = lax.psum_scatter(
        jnp.dot(attended, out_weight, preferred_element_type=jnp.float32).astype(jnp.bfloat16),
        "tensor",
        scatter_dimension=0,
        tiled=True,
    ).astype(jnp.float32)
    mixed_stream = (residual.astype(jnp.float32) + rms_scale(attn_rows) * post_gain).astype(
        jnp.bfloat16
    )
    ffn_input = (rms_scale(mixed_stream.astype(jnp.float32)) * ffn_gain).astype(jnp.bfloat16)
    gathered_rows = lax.all_gather(ffn_input, "tensor", axis=0, tiled=True)
    shard_pair = (
        lax.all_gather(gate_weight, "ctx", axis=0, tiled=True),
        lax.all_gather(up_weight, "ctx", axis=0, tiled=True),
    )
    gate_part = jnp.dot(gathered_rows, shard_pair[0], preferred_element_type=jnp.float32)
    up_part = jnp.dot(gathered_rows, shard_pair[1], preferred_element_type=jnp.float32)
    ffn_hidden = gelu_gate(gate_part, up_part)
    return (mixed_stream, ffn_hidden)


def solution(mesh):
    in_specs = (
        P(("dp", "ctx", "tensor"), None),
        P(("dp", "ctx"), "tensor"),
        P(("dp", "ctx"), "tensor"),
        P(("dp", "ctx"), "tensor"),
        P("dp"),
        P("tensor", None),
        P(),
        P(),
        P("ctx", "tensor"),
        P("ctx", "tensor"),
    )
    out_specs = (P(("dp", "ctx", "tensor"), None), P(("dp", "ctx"), "tensor"))
    return jax.shard_map(
        per_device, mesh=mesh, in_specs=in_specs, out_specs=out_specs, check_vma=False
    )
```

profile of v0, /device:TPU:0, one launch (start us, length us, event | category | flops | bytes accessed | tf_op | source)
XLA Modules:
  0.0 227.5 jit_solution(10332107046243191215)
XLA Ops:
  7.2 0.0 copy-start
  7.2 0.0 reduce-scatter.2.cloned.1.call-start
  7.2 1.0 pad_maximum_fusion
  8.2 3.1 %collective-permute-start = (bf16[2,256,128]{2,1,0:T(8,128)(2,1)S(1)}, bf16[2,256,128]{2,1,0:T(8,128)(2,1)S(1)}, u32[]{:S(2)}, u32[]{:S(2)}) collective-permute-start(bf16[2,256,128]{2,1,0:T(8,128)(2,1)S(1)} %pad_maximum_fusion), channel_id=1, source_target_pairs={{0,1},{1,0},{2,3},{3,2},{4,5},{5,4},{6,7},{7,6},{8,9},{9,8},{10,11... | collective-permute-start | bytes 393224 | tf_op jit(solution)/shard_map/ppermute | solution.py:15
  11.4 0.9 bitcast_convert_fusion
  12.3 0.8 reduce-window.8
  13.1 0.1 convert_reduce_fusion.2
  13.2 0.1 convert_reduce_fusion.1
  13.3 1.5 collective-permute-done
  14.9 1.0 maximum_select_fusion
  15.9 0.6 fusion.34
  16.5 7.3 %all-gather = bf16[1024,1,256]{2,0,1:T(8,128)(2,1)S(1)} all-gather(bf16[256,1,256]{2,0,1:T(8,128)(2,1)S(1)} %pad_maximum_fusion.1), channel_id=2, replica_groups=mesh['dp'=2,'ctx'=4,'tensor'=4] {'ctx'}, dimensions={0}, use_global_device_ids=true | all-gather | bytes 655360 | tf_op jit(solution)/shard_map/all_gather | solution.py:100
  23.9 7.3 %all-gather.1 = bf16[1,1024,256]{2,1,0:T(8,128)(2,1)S(1)} all-gather(bf16[1,256,256]{2,1,0:T(8,128)(2,1)S(1)} %get-tuple-element.8), channel_id=3, replica_groups=mesh['dp'=2,'ctx'=4,'tensor'=4] {'ctx'}, dimensions={1}, use_global_device_ids=true | all-gather | bytes 655360 | tf_op jit(solution)/shard_map/all_gather | solution.py:101
  31.1 0.7 convert_reduce_fusion
  31.8 2.4 %convolution_convert_fusion = bf16[256,3584]{1,0:T(8,128)(2,1)} fusion(bf16[256,3584]{1,0:T(8,128)(2,1)S(1)} %copy-done, bf16[256,1024]{1,0:T(8,128)(2,1)S(1)} %get-tuple-element.13, bf16[1,1024,256]{2,1,0:T(8,128)(2,1)S(1)} %all-gather.1, f32[256]{0:T(256)S(1)} %get-tuple-element.12), kind=kOutput, calls=%fused_computation | convolution fusion | flops 605028352 | bytes 4719616 | tf_op jit(solution)/shard_map/dot_general | solution.py:116
  34.2 0.0 reduce-scatter.2.cloned.1.call-update
  34.2 0.0 all-gather.6.cloned.1.call-start
  34.3 40.2 %reduce-scatter.2.cloned.1.call-done = bf16[64,3584]{1,0:T(8,128)(2,1)} async-done(((bf16[256,3584]{1,0:T(8,128)(2,1)}), bf16[64,3584]{1,0:T(8,128)(2,1)}) %reduce-scatter.2.cloned.1.call-update) | async-done | bytes 458768 | tf_op jit(solution)/shard_map/reduce_scatter | solution.py:115
  74.5 1.2 fusion.8
  75.7 1.4 fusion.12
  77.1 0.0 copy-start.1
  77.2 0.9 fusion.14
  78.1 0.0 all-gather.6.cloned.1.call-update
  78.1 0.0 all-gather.8.cloned.1.call-start
  78.2 0.7 all-gather.8.cloned.1.call-update
  78.9 0.0 all-gather.10.cloned.1.call-start
  78.9 0.5 all-gather.10.cloned.1.call-update
  79.5 39.2 %all-gather.6.cloned.1.call-done = bf16[256,3584]{1,0:T(8,128)(2,1)} async-done(((bf16[64,3584]{1,0:T(8,128)(2,1)}), bf16[256,3584]{1,0:T(8,128)(2,1)}) %all-gather.6.cloned.1.call-update) | async-done | bytes 1835024 | tf_op jit(solution)/shard_map/all_gather | solution.py:125
  118.7 47.5 %all-gather.8.cloned.1.call-done = bf16[3584,896]{1,0:T(8,128)(2,1)} async-done(((bf16[896,896]{1,0:T(8,128)(2,1)}), bf16[3584,896]{1,0:T(8,128)(2,1)}) %all-gather.8.cloned.1.call-update) | async-done | bytes 6422544 | tf_op jit(solution)/shard_map/all_gather | solution.py:127
  166.2 5.5 %fusion.52 = f32[256,896]{1,0:T(8,128)S(1)} fusion(bf16[256,3584]{1,0:T(8,128)(2,1)} %all-gather.6.cloned.1.call-done, bf16[3584,896]{1,0:T(8,128)(2,1)} %all-gather.8.cloned.1.call-done), kind=kOutput, calls=%fused_computation.83 | convolution fusion | flops 1644167168 | bytes 9175040 | tf_op jit(solution)/shard_map/dot_general | solution.py:130
  171.6 43.1 %all-gather.10.cloned.1.call-done = bf16[3584,896]{1,0:T(8,128)(2,1)} async-done(((bf16[896,896]{1,0:T(8,128)(2,1)}), bf16[3584,896]{1,0:T(8,128)(2,1)}) %all-gather.10.cloned.1.call-update) | async-done | bytes 6422544 | tf_op jit(solution)/shard_map/all_gather | solution.py:128
  214.7 6.3 %fusion.5 = bf16[256,896]{1,0:T(8,128)(2,1)} fusion(bf16[256,3584]{1,0:T(8,128)(2,1)} %all-gather.6.cloned.1.call-done, bf16[3584,896]{1,0:T(8,128)(2,1)} %all-gather.10.cloned.1.call-done, f32[256,896]{1,0:T(8,128)S(1)} %fusion.52), kind=kOutput, calls=%fused_computation.9 | convolution fusion | flops 1646460928 | bytes 9633792 | tf_op jit(solution)/shard_map/dot_general | solution.py:131
  (16 shorter events, 0.1 us)
Async XLA Ops:
  7.2 24.7 %copy-start = (bf16[256,3584]{1,0:T(8,128)(2,1)S(1)}, bf16[256,3584]{1,0:T(8,128)(2,1)}, u32[]{:S(2)}) copy-start(bf16[256,3584]{1,0:T(8,128)(2,1)} %param.15) | copy-start | bytes 5505028
  7.2 67.3 %reduce-scatter.2.cloned.1.call-start = ((), (), s32[]{:S(2)}) async-start(), calls=%async_computation.1 | async-start | bytes 2293760 | tf_op jit(solution)/shard_map/reduce_scatter | solution.py:115
  8.2 6.6 %collective-permute-start = (bf16[2,256,128]{2,1,0:T(8,128)(2,1)S(1)}, bf16[2,256,128]{2,1,0:T(8,128)(2,1)S(1)}, u32[]{:S(2)}, u32[]{:S(2)}) collective-permute-start(bf16[2,256,128]{2,1,0:T(8,128)(2,1)S(1)} %pad_maximum_fusion), channel_id=1, source_target_pairs={{0,1},{1,0},{2,3},{3,2},{4,5},{5,4},{6,7},{7,6},{8,9},{9,8},{10,11... | collective-permute-start | bytes 393224 | tf_op jit(solution)/shard_map/ppermute | solution.py:15
  34.2 41.5 %copy-start.2 = (bf16[64,3584]{1,0:T(8,128)(2,1)S(1)}, bf16[64,3584]{1,0:T(8,128)(2,1)}, u32[]{:S(2)}) copy-start(bf16[64,3584]{1,0:T(8,128)(2,1)} %param.10) | copy-start | bytes 1376260
  34.2 41.5 %copy-start.3 = (f32[3584]{0:T(1024)S(1)}, f32[3584]{0:T(1024)}, u32[]{:S(2)}) copy-start(f32[3584]{0:T(1024)} %param.16) | copy-start | bytes 43012
  34.2 43.0 %copy-start.4 = (f32[3584]{0:T(1024)S(1)}, f32[3584]{0:T(1024)}, u32[]{:S(2)}) copy-start(f32[3584]{0:T(1024)} %param.17) | copy-start | bytes 43012
  34.2 84.4 %all-gather.6.cloned.1.call-start = ((), (), s32[]{:S(2)}) async-start(), calls=%async_computation.2 | async-start | bytes 2293760 | tf_op jit(solution)/shard_map/all_gather | solution.py:125
  77.1 2.3 %copy-start.1 = (bf16[64,3584]{1,0:T(8,128)(2,1)}, bf16[64,3584]{1,0:T(8,128)(2,1)S(1)}, u32[]{:S(2)}) copy-start(bf16[64,3584]{1,0:T(8,128)(2,1)S(1)} %get-tuple-element.3) | copy-start | bytes 1376260
  78.1 88.0 %all-gather.8.cloned.1.call-start = ((), (), s32[]{:S(2)}) async-start(), calls=%async_computation.3 | async-start | bytes 8028160 | tf_op jit(solution)/shard_map/all_gather | solution.py:127
  78.9 135.9 %all-gather.10.cloned.1.call-start = ((), (), s32[]{:S(2)}) async-start(), calls=%async_computation.4 | async-start | bytes 8028160 | tf_op jit(solution)/shard_map/all_gather | solution.py:128
Sparse Core Ops, SparseCore 0:
  34.4 40.0 reduce-scatter.1
  78.3 40.3 all-gather.5
  120.2 45.9 all-gather.7
  167.6 47.0 all-gather.9
where the time goes:
time: 228 us
  waiting for transfers between devices  173 us (76%)
  matrix products  14.8 us (6%)
  blocking collectives  14.6 us (6%)
  between operations  13.9 us (6%)
  other arithmetic  8.2 us (4%)
  starting transfers between devices  3.28 us (1%)
    all_gather x1, waiting for transfers between devices, per_device(): lax.all_gather(gate_weight, 'ctx', axis=0, tiled=True)  47.5 us
    all_gather x1, waiting for transfers between devices, per_device(): lax.all_gather(up_weight, 'ctx', axis=0, tiled=True)  43.1 us
    reduce_scatter x1, waiting for transfers between devices, per_device(): lax.psum_scatter(jnp.dot(attended, out_weight, preferred_element_type=jnp...  40.2 us
    all_gather x1, waiting for transfers between devices, per_device(): gathered_rows = lax.all_gather(ffn_input, 'tensor', axis=0, tiled=True)  39.2 us
    all_gather x1, blocking collectives, per_device(): lax.all_gather(key_rot, 'ctx', axis=0, tiled=True)  7.34 us
    all_gather x1, blocking collectives, per_device(): lax.all_gather(joined[1], 'ctx', axis=0, tiled=True)  7.26 us
    dot_general x1, matrix products, per_device(): jnp.dot(gathered_rows, shard_pair[1], preferred_element_type=jnp.float32)  6.25 us
    dot_general x1, matrix products, per_device(): jnp.dot(gathered_rows, shard_pair[0], preferred_element_type=jnp.float32)  5.45 us
  transfers between devices with their start and end apart: 5, of which 5 were waited for; matrix products, arithmetic and copies ran while one was open for 3% of the time, Pallas kernels for 0%

commit v1 on v0

--- a/solution.py
+++ b/solution.py
@@ -122,7 +122,14 @@
         jnp.bfloat16
     )
     ffn_input = (rms_scale(mixed_stream.astype(jnp.float32)) * ffn_gain).astype(jnp.bfloat16)
-    gathered_rows = lax.all_gather(ffn_input, "tensor", axis=0, tiled=True)
+    ring = [ffn_input]
+    for hop in range(3):
+        ring.append(lax.ppermute(ring[-1], "tensor", [(dev, (dev + 1) % 4) for dev in range(4)]))
+    gathered_rows = jnp.roll(
+        jnp.concatenate(ring[::-1], axis=0),
+        (lax.axis_index("tensor") + 1) * ring[0].shape[0],
+        axis=0,
+    )
     shard_pair = (
         lax.all_gather(gate_weight, "ctx", axis=0, tiled=True),
         lax.all_gather(up_weight, "ctx", axis=0, tiled=True),

time: 228 us -> 147 us (0.64)
  waiting for transfers between devices: 173 us -> 81.7 us
  local copies, waits for them, and re-layouts: 0.03 us -> 6.97 us
    all_gather x1, waiting for transfers between devices: 47.5 us -> 2.09 us  [per_device(): lax.all_gather(gate_weight, 'ctx', axis=0, tiled=True)]
    all_gather x1, waiting for transfers between devices: 43.1 us -> 0.01 us  [per_device(): lax.all_gather(up_weight, 'ctx', axis=0, tiled=True)]
    all_gather x1 -> x0, waiting for transfers between devices: 39.2 us -> none  [per_device(): gathered_rows = lax.all_gather(ffn_input, 'tensor', axis=0, tiled=True)]
    ppermute x0 -> x3, waiting for transfers between devices: none -> 38 us  [per_device(): lax.ppermute(ring[-1], 'tensor', [(dev, (dev + 1) % 4) for dev in range(4)])]
    unnamed x10 -> x16, local copies, waits for them, and re-layouts: 0.03 us -> 6.97 us
  transfers between devices with their start and end apart: 5 -> 7, of which waited for: 5 -> 6; matrix products, arithmetic and copies ran while one was open for 3% -> 13% of each run, Pallas kernels for 0% -> 0%
where the time goes in v1:
time: 147 us
  waiting for transfers between devices  81.7 us (56%)
  between operations  15.6 us (11%)
  matrix products  14.9 us (10%)
  blocking collectives  14.6 us (10%)
  other arithmetic  9.35 us (6%)
  local copies, waits for them, and re-layouts  6.97 us (5%)
  starting transfers between devices  3.77 us (3%)
    reduce_scatter x1, waiting for transfers between devices, per_device(): lax.psum_scatter(jnp.dot(attended, out_weight, preferred_element_type=jnp...  39.1 us
    ppermute x3, waiting for transfers between devices, per_device(): lax.ppermute(ring[-1], 'tensor', [(dev, (dev + 1) % 4) for dev in range(4)])  38 us
    all_gather x1, blocking collectives, per_device(): lax.all_gather(key_rot, 'ctx', axis=0, tiled=True)  7.34 us
    all_gather x1, blocking collectives, per_device(): lax.all_gather(joined[1], 'ctx', axis=0, tiled=True)  7.26 us
    unnamed x16, local copies, waits for them, and re-layouts  6.97 us
    dot_general x1, matrix products, per_device(): jnp.dot(gathered_rows, shard_pair[0], preferred_element_type=jnp.float32)  6.39 us
    dot_general x1, matrix products, per_device(): jnp.dot(gathered_rows, shard_pair[1], preferred_element_type=jnp.float32)  5.45 us
    ppermute x1, starting transfers between devices, partner_2(): return lax.ppermute(value, axis, pairs)  3.12 us
  transfers between devices with their start and end apart: 7, of which 6 were waited for; matrix products, arithmetic and copies ran while one was open for 13% of the time, Pallas kernels for 0%

profile of v1, /device:TPU:0, one launch (start us, length us, event | category | flops | bytes accessed | tf_op | source)
XLA Modules:
  0.0 146.9 jit_solution(6752595434864188039)
XLA Ops:
  8.1 1.0 pad_maximum_fusion
  9.1 3.1 %collective-permute-start = (bf16[2,256,128]{2,1,0:T(8,128)(2,1)S(1)}, bf16[2,256,128]{2,1,0:T(8,128)(2,1)S(1)}, u32[]{:S(2)}, u32[]{:S(2)}) collective-permute-start(bf16[2,256,128]{2,1,0:T(8,128)(2,1)S(1)} %pad_maximum_fusion), channel_id=1, source_target_pairs={{0,1},{1,0},{2,3},{3,2},{4,5},{5,4},{6,7},{7,6},{8,9},{9,8},{10,11... | collective-permute-start | bytes 393224 | tf_op jit(solution)/shard_map/ppermute | solution.py:15
  12.2 0.9 bitcast_convert_fusion
  13.1 0.8 reduce-window.8
  14.2 1.5 %collective-permute-done = bf16[2,256,128]{2,1,0:T(8,128)(2,1)S(1)} collective-permute-done((bf16[2,256,128]{2,1,0:T(8,128)(2,1)S(1)}, bf16[2,256,128]{2,1,0:T(8,128)(2,1)S(1)}, u32[]{:S(2)}, u32[]{:S(2)}) %collective-permute-start) | collective-permute-done | bytes 131104 | tf_op jit(solution)/shard_map/ppermute | solution.py:15
  15.7 1.0 maximum_select_fusion
  16.7 0.6 fusion.45
  17.4 7.3 %all-gather = bf16[1024,1,256]{2,0,1:T(8,128)(2,1)S(1)} all-gather(bf16[256,1,256]{2,0,1:T(8,128)(2,1)S(1)} %pad_maximum_fusion.1), channel_id=2, replica_groups=mesh['dp'=2,'ctx'=4,'tensor'=4] {'ctx'}, dimensions={0}, use_global_device_ids=true | all-gather | bytes 655360 | tf_op jit(solution)/shard_map/all_gather | solution.py:100
  24.7 7.3 %all-gather.1 = bf16[1,1024,256]{2,1,0:T(8,128)(2,1)S(1)} all-gather(bf16[1,256,256]{2,1,0:T(8,128)(2,1)S(1)} %get-tuple-element.8), channel_id=3, replica_groups=mesh['dp'=2,'ctx'=4,'tensor'=4] {'ctx'}, dimensions={1}, use_global_device_ids=true | all-gather | bytes 655360 | tf_op jit(solution)/shard_map/all_gather | solution.py:101
  32.0 0.7 convert_reduce_fusion
  32.7 2.4 %convolution_convert_fusion = bf16[256,3584]{1,0:T(8,128)(2,1)} fusion(bf16[256,3584]{1,0:T(8,128)(2,1)S(1)} %copy-done, bf16[256,1024]{1,0:T(8,128)(2,1)S(1)} %get-tuple-element.13, bf16[1,1024,256]{2,1,0:T(8,128)(2,1)S(1)} %all-gather.1, f32[256]{0:T(256)S(1)} %get-tuple-element.12), kind=kOutput, calls=%fused_computation | convolution fusion | flops 605028352 | bytes 4719616 | tf_op jit(solution)/shard_map/dot_general | solution.py:116
  35.1 0.5 all-gather.7.cloned.1.call-update
  35.7 0.5 all-gather.5.cloned.1.call-update
  36.2 39.1 %reduce-scatter.2.cloned.1.call-done = bf16[64,3584]{1,0:T(8,128)(2,1)} async-done(((bf16[256,3584]{1,0:T(8,128)(2,1)}), bf16[64,3584]{1,0:T(8,128)(2,1)}) %reduce-scatter.2.cloned.1.call-update) | async-done | bytes 458768 | tf_op jit(solution)/shard_map/reduce_scatter | solution.py:115
  75.3 1.2 fusion.11
  76.6 1.4 fusion.15
  78.0 0.2 fusion.17
  78.2 0.5 collective-permute-start.1
  78.7 13.2 %collective-permute-done.1 = bf16[64,3584]{1,0:T(8,128)(2,1)S(1)} collective-permute-done((bf16[64,3584]{1,0:T(8,128)(2,1)S(1)}, bf16[64,3584]{1,0:T(8,128)(2,1)S(1)}, u32[]{:S(2)}, u32[]{:S(2)}) %collective-permute-start.1) | collective-permute-done | bytes 458784 | tf_op jit(solution)/shard_map/ppermute | solution.py:127
  91.9 12.8 %collective-permute-done.2 = bf16[64,3584]{1,0:T(8,128)(2,1)S(1)} collective-permute-done((bf16[64,3584]{1,0:T(8,128)(2,1)S(1)}, bf16[64,3584]{1,0:T(8,128)(2,1)S(1)}, u32[]{:S(2)}, u32[]{:S(2)}) %collective-permute-start.2) | collective-permute-done | bytes 458784 | tf_op jit(solution)/shard_map/ppermute | solution.py:127
  104.7 12.0 %collective-permute-done.3 = bf16[64,3584]{1,0:T(8,128)(2,1)} collective-permute-done((bf16[64,3584]{1,0:T(8,128)(2,1)S(1)}, bf16[64,3584]{1,0:T(8,128)(2,1)}, u32[]{:S(2)}, u32[]{:S(2)}) %collective-permute-start.3) | collective-permute-done | bytes 458784 | tf_op jit(solution)/shard_map/ppermute | solution.py:127
  116.7 1.8 %constant_dynamic-update-slice_fusion.7 = bf16[512,3584]{1,0:T(8,128)(2,1)} fusion(bf16[64,3584]{1,0:T(8,128)(2,1)} %collective-permute-done.3), kind=kLoop, calls=%fused_computation.75 | loop fusion | bytes 917504
  118.6 0.8 constant_dynamic-update-slice_fusion.6
  119.4 0.8 constant_dynamic-update-slice_fusion.5
  120.2 0.9 constant_dynamic-update-slice_fusion.4
  121.1 1.8 %constant_dynamic-update-slice_fusion.3 = bf16[512,3584]{1,0:T(8,128)(2,1)} fusion(bf16[512,3584]{1,0:T(8,128)(2,1)} %constant_dynamic-update-slice_fusion.4, bf16[64,3584]{1,0:T(8,128)(2,1)} %collective-permute-done.3), kind=kLoop, calls=%fused_computation.71 | loop fusion | bytes 917504
  123.0 0.8 constant_dynamic-update-slice_fusion.2
  123.8 0.8 constant_dynamic-update-slice_fusion.1
  124.6 1.0 constant_dynamic-update-slice_fusion
  125.6 5.5 %fusion = f32[256,896]{1,0:T(8,128)S(1)} fusion(bf16[3584,896]{1,0:T(8,128)(2,1)} %all-gather.7.cloned.1.call-done, bf16[512,3584]{1,0:T(8,128)(2,1)} %constant_dynamic-update-slice_fusion, s32[]{:T(128)S(6)} %select_n.58), kind=kOutput, calls=%fused_computation.1 | convolution fusion | flops 1644167168 | bytes 9175044 | tf_op jit(solution)/shard_map/dot_general | solution.py:138
  131.0 2.1 %all-gather.5.cloned.1.call-done = bf16[3584,896]{1,0:T(8,128)(2,1)} async-done(((bf16[896,896]{1,0:T(8,128)(2,1)}), bf16[3584,896]{1,0:T(8,128)(2,1)}) %all-gather.5.cloned.1.call-update) | async-done | bytes 6422544 | tf_op jit(solution)/shard_map/all_gather | solution.py:134
  133.1 6.4 %fusion.30 = bf16[256,896]{1,0:T(8,128)(2,1)} fusion(f32[256,896]{1,0:T(8,128)S(1)} %fusion, bf16[3584,896]{1,0:T(8,128)(2,1)} %all-gather.5.cloned.1.call-done, bf16[512,3584]{1,0:T(8,128)(2,1)} %constant_dynamic-update-slice_fusion, s32[]{:T(128)S(6)} %select_n.58), kind=kOutput, calls=%fused_computation.36 | convolution fusion | flops 1646460928 | bytes 9633796 | tf_op jit(solution)/shard_map/dot_general | solution.py:137
  (27 shorter events, 0.4 us)
Async XLA Ops:
  8.0 24.7 %copy-start = (bf16[256,3584]{1,0:T(8,128)(2,1)S(1)}, bf16[256,3584]{1,0:T(8,128)(2,1)}, u32[]{:S(2)}) copy-start(bf16[256,3584]{1,0:T(8,128)(2,1)} %param.15) | copy-start | bytes 5505028
  8.0 67.3 %reduce-scatter.2.cloned.1.call-start = ((), (), s32[]{:S(2)}) async-start(), calls=%async_computation.1 | async-start | bytes 2293760 | tf_op jit(solution)/shard_map/reduce_scatter | solution.py:115
  9.1 6.6 %collective-permute-start = (bf16[2,256,128]{2,1,0:T(8,128)(2,1)S(1)}, bf16[2,256,128]{2,1,0:T(8,128)(2,1)S(1)}, u32[]{:S(2)}, u32[]{:S(2)}) collective-permute-start(bf16[2,256,128]{2,1,0:T(8,128)(2,1)S(1)} %pad_maximum_fusion), channel_id=1, source_target_pairs={{0,1},{1,0},{2,3},{3,2},{4,5},{5,4},{6,7},{7,6},{8,9},{9,8},{10,11... | collective-permute-start | bytes 393224 | tf_op jit(solution)/shard_map/ppermute | solution.py:15
  35.0 41.5 %copy-start.2 = (bf16[64,3584]{1,0:T(8,128)(2,1)S(1)}, bf16[64,3584]{1,0:T(8,128)(2,1)}, u32[]{:S(2)}) copy-start(bf16[64,3584]{1,0:T(8,128)(2,1)} %param.10) | copy-start | bytes 1376260
  35.0 41.5 %copy-start.4 = (f32[3584]{0:T(1024)S(1)}, f32[3584]{0:T(1024)}, u32[]{:S(2)}) copy-start(f32[3584]{0:T(1024)} %param.16) | copy-start | bytes 43012
  35.0 43.0 %copy-start.3 = (f32[3584]{0:T(1024)S(1)}, f32[3584]{0:T(1024)}, u32[]{:S(2)}) copy-start(f32[3584]{0:T(1024)} %param.17) | copy-start | bytes 43012
  35.1 90.5 %all-gather.7.cloned.1.call-start = ((), (), s32[]{:S(2)}) async-start(), calls=%async_computation.3 | async-start | bytes 8028160 | tf_op jit(solution)/shard_map/all_gather | solution.py:135
  35.6 97.5 %all-gather.5.cloned.1.call-start = ((), (), s32[]{:S(2)}) async-start(), calls=%async_computation.2 | async-start | bytes 8028160 | tf_op jit(solution)/shard_map/all_gather | solution.py:134
  78.0 46.6 %copy-start.1 = (bf16[64,3584]{1,0:T(8,128)(2,1)}, bf16[64,3584]{1,0:T(8,128)(2,1)S(1)}, u32[]{:S(2)}) copy-start(bf16[64,3584]{1,0:T(8,128)(2,1)S(1)} %get-tuple-element.3) | copy-start | bytes 1376260
  78.2 13.7 %collective-permute-start.1 = (bf16[64,3584]{1,0:T(8,128)(2,1)S(1)}, bf16[64,3584]{1,0:T(8,128)(2,1)S(1)}, u32[]{:S(2)}, u32[]{:S(2)}) collective-permute-start(bf16[64,3584]{1,0:T(8,128)(2,1)S(1)} %fusion.17), channel_id=1, source_target_pairs={{0,1},{1,2},{2,3},{3,0},{4,5},{5,6},{6,7},{7,4},{8,9},{9,10},{10,1... | collective-permute-start | bytes 1376264 | tf_op jit(solution)/shard_map/ppermute | solution.py:127
  91.9 12.8 %collective-permute-start.2 = (bf16[64,3584]{1,0:T(8,128)(2,1)S(1)}, bf16[64,3584]{1,0:T(8,128)(2,1)S(1)}, u32[]{:S(2)}, u32[]{:S(2)}) collective-permute-start(bf16[64,3584]{1,0:T(8,128)(2,1)S(1)} %collective-permute-done.1), channel_id=1, source_target_pairs={{0,1},{1,2},{2,3},{3,0},{4,5},{5,6},{6,7},{7,4},{8,9},{9,10},{10,1... | collective-permute-start | bytes 1376264 | tf_op jit(solution)/shard_map/ppermute | solution.py:127
  104.7 12.0 %collective-permute-start.3 = (bf16[64,3584]{1,0:T(8,128)(2,1)S(1)}, bf16[64,3584]{1,0:T(8,128)(2,1)}, u32[]{:S(2)}, u32[]{:S(2)}) collective-permute-start(bf16[64,3584]{1,0:T(8,128)(2,1)S(1)} %collective-permute-done.2), channel_id=1, source_target_pairs={{0,1},{1,2},{2,3},{3,0},{4,5},{5,6},{6,7},{7,4},{8,9},{9,10},{10,1... | collective-permute-start | bytes 1376264 | tf_op jit(solution)/shard_map/ppermute | solution.py:127
Sparse Core Ops, SparseCore 0:
  35.2 40.0 reduce-scatter.1
Sparse Core Ops, SparseCore 1:
  37.1 47.5 all-gather.6
  86.1 46.9 all-gather.4
